TPU v7x, 32 devices: a whole 2x2x4 slice. The times are simulated.
32 devices in a mesh: worker: 8 (over z, y), mp: 4 (over x, core).
Axes of the slice: x: 2, y: 2, z: 4, core: 2. Of those that a mesh axis runs over, the one named last changes fastest.
Arguments:
- gradients: bfloat16 [128, 1048576], P('worker', 'mp'), may hold values from -30 to 30
- center: float32 [1048576], P('mp'), may hold values from -6 to 6
- outside_sq: float32 [3, 128], P(None, 'worker'), may hold values from 209715.2 to 2097152
- radius: float32 [3], replicated, may hold values from 1.5 to 3
Outputs:
- new_center: float32 [1048576], P('mp')
- norms: float32 [128], P('worker')
All inputs are finite; a program needn't handle non-finite values.
Results may differ from a plain program's by a relative error of at most 0.0003.
Values sent between devices are 32-bit elements; how exact they have to be, the bound alone decides.
No kernel may reach another device: no remote copies, remote signals or barrier semaphores. Data moves between devices by JAX's collectives and lax.ppermute only.
A program may use at most 64 MiB of HBM per device.

v0:
```python
import jax
import jax.numpy as jnp
from jax import lax
from jax.sharding import PartitionSpec as P

ITERS = 3


def shards(gradients, center, outside_sq, radius):
    workers_all = gradients.shape[0] * lax.axis_size("worker")
    root_total = jnp.sqrt(jnp.float32(center.shape[0] * lax.axis_size("mp")))
    value = center
    norms = jnp.zeros((gradients.shape[0],), jnp.float32)
    for step in range(ITERS):
        diff = gradients.astype(jnp.float32) - value[None, :]
        partial_value = jnp.sum(diff * diff, axis=1)
        squared = lax.psum(partial_value, "mp") + outside_sq[step]
        norms = jnp.sqrt(squared)
        factor = jnp.minimum(jnp.float32(1.0), radius[step] * root_total / norms)
        local = jnp.sum(factor[:, None] * diff, axis=0)
        summed = lax.psum(local, "worker")
        value = value + summed / jnp.float32(workers_all)
    return (value, norms)


def solution(mesh):
    placed = (P("worker", "mp"), P("mp"), P(None, "worker"), P())
    return jax.shard_map(
        shards, mesh=mesh, in_specs=placed, out_specs=(P("mp"), P("worker")), check_vma=False
    )
```

profile of v0, /device:TPU:0, one launch (start us, length us, event | category | flops | bytes accessed | tf_op | source)
XLA Modules:
  0.0 333.9 jit_solution(5382687448233932146)
XLA Ops:
  7.2 0.0 copy-start
  7.2 0.0 copy-start.1
  7.2 0.0 copy-start.2
  7.2 0.0 all-reduce.4.cloned.1.call-start
  7.2 5.5 %fusion.10 = f32[16]{0:T(128)S(1)} fusion(bf16[16,262144]{1,0:T(8,128)(2,1)} %param.4, f32[262144]{0:T(1024)} %param.5), kind=kLoop, calls=%fused_computation.13 | loop fusion | flops 16777200 | bytes 9437248 | tf_op jit(solution)/shard_map/reduce_sum | solution.py:16
  12.8 8.4 %psum.42 = f32[16]{0:T(128)S(1)} all-reduce(f32[16]{0:T(128)S(1)} %fusion.10), channel_id=1, replica_groups=mesh['worker'=8,'mp'=4] {'mp'}, use_global_device_ids=true, to_apply=%region_1.0 | all-reduce | flops 16 | bytes 128 | tf_op jit(solution)/shard_map/psum | solution.py:17
  21.1 0.0 copy-done.1
  21.1 0.7 fusion.20
  22.5 0.0 copy-done.2
  22.5 0.0 copy-done
  22.5 14.0 %fusion.11 = f32[262144]{0:T(1024)} fusion(bf16[16,262144]{1,0:T(8,128)(2,1)} %param.4, f32[16]{0:T(128)S(1)} %fusion.17, f32[262144]{0:T(1024)S(1)} %copy-done), kind=kLoop, calls=%fused_computation.14 | loop fusion | flops 16515072 | bytes 10485824 | tf_op jit(solution)/shard_map/reduce_sum | solution.py:20
  36.5 0.0 all-reduce.4.cloned.1.call-update
  36.5 0.0 all-reduce.6.cloned.1.call-start
  37.2 78.1 %all-reduce.4.cloned.1.call-done = f32[262144]{0:T(1024)} async-done(((f32[262144]{0:T(1024)}), f32[262144]{0:T(1024)}) %all-reduce.4.cloned.1.call-update) | async-done | bytes 1048592 | tf_op jit(solution)/shard_map/psum | solution.py:21
  115.4 1.3 multiply_add_fusion.2
  116.7 5.2 %fusion.8 = f32[16]{0:T(128)S(1)} fusion(bf16[16,262144]{1,0:T(8,128)(2,1)} %param.4, f32[262144]{0:T(1024)S(1)} %multiply_add_fusion.2), kind=kLoop, calls=%fused_computation.11 | loop fusion | flops 16777200 | bytes 9437248 | tf_op jit(solution)/shard_map/reduce_sum | solution.py:16
  121.9 6.5 %psum.44 = f32[16]{0:T(128)S(1)} all-reduce(f32[16]{0:T(128)S(1)} %fusion.8), channel_id=1, replica_groups=mesh['worker'=8,'mp'=4] {'mp'}, use_global_device_ids=true, to_apply=%region_5.0 | all-reduce | flops 16 | bytes 128 | tf_op jit(solution)/shard_map/psum | solution.py:17
  128.4 14.0 %fusion.9 = f32[262144]{0:T(1024)} fusion(bf16[16,262144]{1,0:T(8,128)(2,1)} %param.4, f32[16]{0:T(128)S(1)} %fusion.18, f32[262144]{0:T(1024)S(1)} %multiply_add_fusion.2), kind=kLoop, calls=%fused_computation.12 | loop fusion | flops 16515072 | bytes 10485824 | tf_op jit(solution)/shard_map/reduce_sum | solution.py:20
  142.4 0.0 all-reduce.6.cloned.1.call-update
  142.4 0.0 all-reduce.8.cloned.1.call-start
  143.1 76.9 %all-reduce.6.cloned.1.call-done = f32[262144]{0:T(1024)} async-done(((f32[262144]{0:T(1024)}), f32[262144]{0:T(1024)}) %all-reduce.6.cloned.1.call-update) | async-done | bytes 1048592 | tf_op jit(solution)/shard_map/psum | solution.py:21
  220.0 1.3 multiply_add_fusion.1
  221.3 5.2 %fusion.6 = f32[16]{0:T(128)S(1)} fusion(bf16[16,262144]{1,0:T(8,128)(2,1)} %param.4, f32[262144]{0:T(1024)S(1)} %multiply_add_fusion.1), kind=kLoop, calls=%fused_computation.9 | loop fusion | flops 16777200 | bytes 9437248 | tf_op jit(solution)/shard_map/reduce_sum | solution.py:16
  226.5 6.5 %psum.46 = f32[16]{0:T(128)S(1)} all-reduce(f32[16]{0:T(128)S(1)} %fusion.6), channel_id=1, replica_groups=mesh['worker'=8,'mp'=4] {'mp'}, use_global_device_ids=true, to_apply=%region_9.0 | all-reduce | flops 16 | bytes 128 | tf_op jit(solution)/shard_map/psum | solution.py:17
  233.0 0.5 divide_minimum_fusion
  233.5 14.0 %fusion.7 = f32[262144]{0:T(1024)} fusion(bf16[16,262144]{1,0:T(8,128)(2,1)} %param.4, f32[16]{0:T(128)S(1)} %get-tuple-element.2, f32[262144]{0:T(1024)S(1)} %multiply_add_fusion.1), kind=kLoop, calls=%fused_computation.10 | loop fusion | flops 16515072 | bytes 10485824 | tf_op jit(solution)/shard_map/reduce_sum | solution.py:20
  247.5 0.0 all-reduce.8.cloned.1.call-update
  247.5 77.6 %all-reduce.8.cloned.1.call-done = f32[262144]{0:T(1024)} async-done(((f32[262144]{0:T(1024)}), f32[262144]{0:T(1024)}) %all-reduce.8.cloned.1.call-update) | async-done | bytes 1048592 | tf_op jit(solution)/shard_map/psum | solution.py:21
  325.1 2.3 multiply_add_fusion
  (2 shorter events, 0.0 us)
Async XLA Ops:
  7.2 15.3 %copy-start = (f32[262144]{0:T(1024)S(1)}, f32[262144]{0:T(1024)}, u32[]{:S(2)}) copy-start(f32[262144]{0:T(1024)} %param.5) | copy-start | bytes 3145732
  7.2 14.0 %copy-start.1 = (f32[3]{0:T(128)S(1)}, f32[3]{0:T(128)}, u32[]{:S(2)}) copy-start(f32[3]{0:T(128)} %param.7) | copy-start | bytes 40
  7.2 15.3 %copy-start.2 = (f32[3,16]{1,0:T(4,128)S(1)}, f32[3,16]{1,0:T(4,128)}, u32[]{:S(2)}) copy-start(f32[3,16]{1,0:T(4,128)} %param.6) | copy-start | bytes 580
  7.2 108.2 %all-reduce.4.cloned.1.call-start = ((), (), s32[]{:S(2)}) async-start(), calls=%async_computation | async-start | bytes 2097152 | tf_op jit(solution)/shard_map/psum | solution.py:21
  36.5 183.5 %all-reduce.6.cloned.1.call-start = ((), (), s32[]{:S(2)}) async-start(), calls=%async_computation.1 | async-start | bytes 2097152 | tf_op jit(solution)/shard_map/psum | solution.py:21
  142.4 182.7 %all-reduce.8.cloned.1.call-start = ((), (), s32[]{:S(2)}) async-start(), calls=%async_computation.2 | async-start | bytes 2097152 | tf_op jit(solution)/shard_map/psum | solution.py:21
Sparse Core Ops, SparseCore 0:
  36.6 78.7 all-reduce.3
  142.5 77.4 all-reduce.5
  247.6 77.4 all-reduce.7
where the time goes:
time: 334 us
  waiting for transfers between devices  233 us (70%)
  other arithmetic  63.3 us (19%)
  blocking collectives  21.4 us (6%)
  between operations  15.8 us (5%)
    psum x3, waiting for transfers between devices, shards(): summed = lax.psum(local, 'worker')  233 us
    reduce_sum x3, other arithmetic, shards(): local = jnp.sum(factor[:, None] * diff, axis=0)  41.9 us
    psum x3, blocking collectives, shards(): squared = lax.psum(partial_value, 'mp') + outside_sq[step]  21.4 us
    reduce_sum x3, other arithmetic, shards(): partial_value = jnp.sum(diff * diff, axis=1)  15.9 us
  transfers between devices with their start and end apart: 3, of which 3 were waited for; matrix products, arithmetic and copies ran while one was open for 0% of the time, Pallas kernels for 0%

commit v1 on v0

--- a/solution.py
+++ b/solution.py
@@ -18,7 +18,15 @@
         norms = jnp.sqrt(squared)
         factor = jnp.minimum(jnp.float32(1.0), radius[step] * root_total / norms)
         local = jnp.sum(factor[:, None] * diff, axis=0)
-        summed = lax.psum(local, "worker")
+        total_devices = lax.axis_size("worker")
+        summed, far_arr = (local, 0)
+        while 1 << far_arr < total_devices:
+            by_rank = []
+            for b in range(total_devices):
+                by_rank.append((b, b ^ 1 << far_arr))
+            q_next = lax.ppermute(summed, "worker", by_rank)
+            summed = summed + q_next
+            far_arr = far_arr + 1
         value = value + summed / jnp.float32(workers_all)
     return (value, norms)
 

time: 334 us -> 359 us (1.075)
  waiting for transfers between devices: 233 us -> 266 us
  between operations: 15.8 us -> 2.8 us
  starting transfers between devices: 0.12 us -> 12.4 us
  other arithmetic: 63.3 us -> 52.4 us
    ppermute x0 -> x9, waiting for transfers between devices: none -> 266 us  [shards(): q_next = lax.ppermute(summed, 'worker', by_rank)]
    psum x3 -> x0, waiting for transfers between devices: 233 us -> none  [shards(): summed = lax.psum(local, 'worker')]
    ppermute x0 -> x9, starting transfers between devices: none -> 12.4 us  [shards(): q_next = lax.ppermute(summed, 'worker', by_rank)]
    reduce_sum x3, other arithmetic: 15.9 us -> 10.2 us  [shards(): partial_value = jnp.sum(diff * diff, axis=1)]
  transfers between devices with their start and end apart: 3 -> 9, of which waited for: 3 -> 9; matrix products, arithmetic and copies ran while one was open for 0% -> 0% of each run, Pallas kernels for 0% -> 0%
where the time goes in v1:
time: 359 us; the launch traced here: 358 us
  waiting for transfers between devices  266 us (74%)
  other arithmetic  52.4 us (15%)
  blocking collectives  24.5 us (7%)
  starting transfers between devices  12.4 us (3%)
    ppermute x9, waiting for transfers between devices, shards(): q_next = lax.ppermute(summed, 'worker', by_rank)  266 us
    reduce_sum x3, other arithmetic, shards(): local = jnp.sum(factor[:, None] * diff, axis=0)  39.3 us
    psum x3, blocking collectives, shards(): squared = lax.psum(partial_value, 'mp') + outside_sq[step]  24.5 us
    ppermute x9, starting transfers between devices, shards(): q_next = lax.ppermute(summed, 'worker', by_rank)  12.4 us
    reduce_sum x3, other arithmetic, shards(): partial_value = jnp.sum(diff * diff, axis=1)  10.2 us
  transfers between devices with their start and end apart: 9, of which 9 were waited for; matrix products, arithmetic and copies ran while one was open for 0% of the time, Pallas kernels for 0%

profile of v1, /device:TPU:0, one launch (start us, length us, event | category | flops | bytes accessed | tf_op | source)
XLA Modules:
  0.0 358.5 jit_solution(3368263335349401771)
XLA Ops:
  0.6 0.0 copy-start
  0.6 0.0 copy-start.1
  0.7 0.0 copy-start.2
  0.7 5.5 %fusion.10 = f32[16]{0:T(128)S(1)} fusion(bf16[16,262144]{1,0:T(8,128)(2,1)} %param.4, f32[262144]{0:T(1024)} %param.5), kind=kLoop, calls=%fused_computation.13 | loop fusion | flops 16777200 | bytes 9437248 | tf_op jit(solution)/shard_map/reduce_sum | solution.py:16
  6.2 8.4 %psum.21 = f32[16]{0:T(128)S(1)} all-reduce(f32[16]{0:T(128)S(1)} %fusion.10), channel_id=1, replica_groups=mesh['worker'=8,'mp'=4] {'mp'}, use_global_device_ids=true, to_apply=%region_1.0 | all-reduce | flops 16 | bytes 128 | tf_op jit(solution)/shard_map/psum | solution.py:17
  14.6 0.0 copy-done.1
  14.6 0.7 fusion.20
  15.9 0.0 copy-done.2
  15.9 0.0 copy-done
  15.9 0.0 slice-start
  15.9 13.1 %fusion.11 = f32[262144]{0:T(1024)S(1)} fusion(bf16[16,262144]{1,0:T(8,128)(2,1)} %param.4, f32[16]{0:T(128)S(1)} %fusion.17, f32[262144]{0:T(1024)S(1)} %copy-done), kind=kLoop, calls=%fused_computation.14 | loop fusion | flops 16515072 | bytes 10485824 | tf_op jit(solution)/shard_map/reduce_sum | solution.py:20
  29.1 0.0 slice-start.1
  29.1 1.6 collective-permute-start
  30.7 22.0 %collective-permute-done = f32[262144]{0:T(1024)S(1)} collective-permute-done((f32[262144]{0:T(1024)S(1)}, f32[262144]{0:T(1024)S(1)}, u32[]{:S(2)}, u32[]{:S(2)}) %collective-permute-start) | collective-permute-done | bytes 1048608 | tf_op jit(solution)/shard_map/ppermute | solution.py:27
  52.7 0.1 add.52
  52.9 1.8 collective-permute-start.1
  54.6 21.1 %collective-permute-done.1 = f32[262144]{0:T(1024)S(1)} collective-permute-done((f32[262144]{0:T(1024)S(1)}, f32[262144]{0:T(1024)S(1)}, u32[]{:S(2)}, u32[]{:S(2)}) %collective-permute-start.1) | collective-permute-done | bytes 1048608 | tf_op jit(solution)/shard_map/ppermute | solution.py:27
  75.7 0.1 add.53
  75.8 3.2 collective-permute-start.2
  79.8 41.6 %collective-permute-done.2 = f32[262144]{0:T(1024)S(1)} collective-permute-done((f32[262144]{0:T(1024)S(1)}, f32[262144]{0:T(1024)S(1)}, u32[]{:S(2)}, u32[]{:S(2)}) %collective-permute-start.2) | collective-permute-done | bytes 1048608 | tf_op jit(solution)/shard_map/ppermute | solution.py:27
  121.4 0.2 multiply_add_fusion.2
  121.6 0.0 slice-done
  121.6 0.0 slice-done.1
  121.7 2.3 fusion.8
  124.0 8.4 %psum.22 = f32[16]{0:T(128)S(1)} all-reduce(f32[16]{0:T(128)S(1)} %fusion.8), channel_id=1, replica_groups=mesh['worker'=8,'mp'=4] {'mp'}, use_global_device_ids=true, to_apply=%region_4.0 | all-reduce | flops 16 | bytes 128 | tf_op jit(solution)/shard_map/psum | solution.py:17
  132.4 0.0 slice-start.2
  132.4 13.1 %fusion.9 = f32[262144]{0:T(1024)S(1)} fusion(bf16[16,262144]{1,0:T(8,128)(2,1)} %param.4, f32[16]{0:T(128)S(1)} %fusion.18, f32[262144]{0:T(1024)S(1)} %multiply_add_fusion.2), kind=kLoop, calls=%fused_computation.12 | loop fusion | flops 16515072 | bytes 10485824 | tf_op jit(solution)/shard_map/reduce_sum | solution.py:20
  145.6 0.0 slice-start.3
  145.6 1.1 collective-permute-start.3
  146.6 23.4 %collective-permute-done.3 = f32[262144]{0:T(1024)S(1)} collective-permute-done((f32[262144]{0:T(1024)S(1)}, f32[262144]{0:T(1024)S(1)}, u32[]{:S(2)}, u32[]{:S(2)}) %collective-permute-start.3) | collective-permute-done | bytes 1048608 | tf_op jit(solution)/shard_map/ppermute | solution.py:27
  170.1 0.1 add.57
  170.2 0.5 collective-permute-start.4
  170.7 23.2 %collective-permute-done.4 = f32[262144]{0:T(1024)S(1)} collective-permute-done((f32[262144]{0:T(1024)S(1)}, f32[262144]{0:T(1024)S(1)}, u32[]{:S(2)}, u32[]{:S(2)}) %collective-permute-start.4) | collective-permute-done | bytes 1048608 | tf_op jit(solution)/shard_map/ppermute | solution.py:27
  193.9 0.1 add.58
  194.0 1.3 collective-permute-start.5
  195.9 43.8 %collective-permute-done.5 = f32[262144]{0:T(1024)S(1)} collective-permute-done((f32[262144]{0:T(1024)S(1)}, f32[262144]{0:T(1024)S(1)}, u32[]{:S(2)}, u32[]{:S(2)}) %collective-permute-start.5) | collective-permute-done | bytes 1048608 | tf_op jit(solution)/shard_map/ppermute | solution.py:27
  239.7 0.2 multiply_add_fusion.1
  240.0 0.0 slice-done.2
  240.0 0.0 slice-done.3
  240.0 2.3 fusion.6
  242.4 7.7 %psum.23 = f32[16]{0:T(128)S(1)} all-reduce(f32[16]{0:T(128)S(1)} %fusion.6), channel_id=1, replica_groups=mesh['worker'=8,'mp'=4] {'mp'}, use_global_device_ids=true, to_apply=%region_7.0 | all-reduce | flops 16 | bytes 128 | tf_op jit(solution)/shard_map/psum | solution.py:17
  250.0 0.5 divide_minimum_fusion
  250.6 13.0 %fusion.7 = f32[262144]{0:T(1024)S(1)} fusion(bf16[16,262144]{1,0:T(8,128)(2,1)} %param.4, f32[16]{0:T(128)S(1)} %get-tuple-element.2, f32[262144]{0:T(1024)S(1)} %multiply_add_fusion.1), kind=kLoop, calls=%fused_computation.10 | loop fusion | flops 16515072 | bytes 10485824 | tf_op jit(solution)/shard_map/reduce_sum | solution.py:20
  263.6 1.1 collective-permute-start.6
  264.6 23.3 %collective-permute-done.6 = f32[262144]{0:T(1024)S(1)} collective-permute-done((f32[262144]{0:T(1024)S(1)}, f32[262144]{0:T(1024)S(1)}, u32[]{:S(2)}, u32[]{:S(2)}) %collective-permute-start.6) | collective-permute-done | bytes 1048608 | tf_op jit(solution)/shard_map/ppermute | solution.py:27
  287.9 0.1 add.62
  288.0 0.5 collective-permute-start.7
  288.5 23.0 %collective-permute-done.7 = f32[262144]{0:T(1024)S(1)} collective-permute-done((f32[262144]{0:T(1024)S(1)}, f32[262144]{0:T(1024)S(1)}, u32[]{:S(2)}, u32[]{:S(2)}) %collective-permute-start.7) | collective-permute-done | bytes 1048608 | tf_op jit(solution)/shard_map/ppermute | solution.py:27
  311.5 0.1 add.63
  311.6 1.5 collective-permute-start.8
  313.1 44.2 %collective-permute-done.8 = f32[262144]{0:T(1024)S(1)} collective-permute-done((f32[262144]{0:T(1024)S(1)}, f32[262144]{0:T(1024)S(1)}, u32[]{:S(2)}, u32[]{:S(2)}) %collective-permute-start.8) | collective-permute-done | bytes 1048608 | tf_op jit(solution)/shard_map/ppermute | solution.py:27
  357.2 1.2 multiply_add_fusion
  (4 shorter events, 0.0 us)
Async XLA Ops:
  0.6 15.3 %copy-start = (f32[262144]{0:T(1024)S(1)}, f32[262144]{0:T(1024)}, u32[]{:S(2)}) copy-start(f32[262144]{0:T(1024)} %param.5) | copy-start | bytes 3145732
  0.6 13.9 %copy-start.1 = (f32[3]{0:T(128)S(1)}, f32[3]{0:T(128)}, u32[]{:S(2)}) copy-start(f32[3]{0:T(128)} %param.7) | copy-start | bytes 40
  0.7 15.2 %copy-start.2 = (f32[3,16]{1,0:T(4,128)S(1)}, f32[3,16]{1,0:T(4,128)}, u32[]{:S(2)}) copy-start(f32[3,16]{1,0:T(4,128)} %param.6) | copy-start | bytes 580
  15.9 105.7 %slice-start = ((s8[8388608]{0:T(1024)(128)(4,1)}), s8[4194304]{0:T(1024)(128)(4,1)S(1)}, s32[]{:S(2)}) async-start(s8[8388608]{0:T(1024)(128)(4,1)} %bitcast.24), calls=%async_computation | async-start | bytes 8388608
  29.1 92.6 %slice-start.1 = ((s8[8388608]{0:T(1024)(128)(4,1)}), s8[4194304]{0:T(1024)(128)(4,1)S(1)}, s32[]{:S(2)}) async-start(s8[8388608]{0:T(1024)(128)(4,1)} %bitcast.24), calls=%async_computation.1 | async-start | bytes 8388608
  29.1 23.6 %collective-permute-start = (f32[262144]{0:T(1024)S(1)}, f32[262144]{0:T(1024)S(1)}, u32[]{:S(2)}, u32[]{:S(2)}) collective-permute-start(f32[262144]{0:T(1024)S(1)} %fusion.11), channel_id=1, source_target_pairs={{0,4},{4,0},{8,12},{12,8},{16,20},{20,16},{24,28},{28,24},{1,5},{5... | collective-permute-start | bytes 3145736 | tf_op jit(solution)/shard_map/ppermute | solution.py:27
  52.9 22.9 %collective-permute-start.1 = (f32[262144]{0:T(1024)S(1)}, f32[262144]{0:T(1024)S(1)}, u32[]{:S(2)}, u32[]{:S(2)}) collective-permute-start(f32[262144]{0:T(1024)S(1)} %add.52), channel_id=1, source_target_pairs={{0,8},{4,12},{8,0},{12,4},{16,24},{20,28},{24,16},{28,20},{1,9},{5... | collective-permute-start | bytes 3145736 | tf_op jit(solution)/shard_map/ppermute | solution.py:27
  75.8 45.5 %collective-permute-start.2 = (f32[262144]{0:T(1024)S(1)}, f32[262144]{0:T(1024)S(1)}, u32[]{:S(2)}, u32[]{:S(2)}) collective-permute-start(f32[262144]{0:T(1024)S(1)} %add.53), channel_id=1, source_target_pairs={{0,16},{4,20},{8,24},{12,28},{16,0},{20,4},{24,8},{28,12},{1,17},{... | collective-permute-start | bytes 3145736 | tf_op jit(solution)/shard_map/ppermute | solution.py:27
  132.4 107.6 %slice-start.2 = ((s8[8388608]{0:T(1024)(128)(4,1)}), s8[4194304]{0:T(1024)(128)(4,1)S(1)}, s32[]{:S(2)}) async-start(s8[8388608]{0:T(1024)(128)(4,1)} %bitcast.26), calls=%async_computation.2 | async-start | bytes 8388608
  145.6 94.4 %slice-start.3 = ((s8[8388608]{0:T(1024)(128)(4,1)}), s8[4194304]{0:T(1024)(128)(4,1)S(1)}, s32[]{:S(2)}) async-start(s8[8388608]{0:T(1024)(128)(4,1)} %bitcast.26), calls=%async_computation.3 | async-start | bytes 8388608
  145.6 24.5 %collective-permute-start.3 = (f32[262144]{0:T(1024)S(1)}, f32[262144]{0:T(1024)S(1)}, u32[]{:S(2)}, u32[]{:S(2)}) collective-permute-start(f32[262144]{0:T(1024)S(1)} %fusion.9), channel_id=1, source_target_pairs={{0,4},{4,0},{8,12},{12,8},{16,20},{20,16},{24,28},{28,24},{1,5},{5... | collective-permute-start | bytes 3145736 | tf_op jit(solution)/shard_map/ppermute | solution.py:27
  170.2 23.6 %collective-permute-start.4 = (f32[262144]{0:T(1024)S(1)}, f32[262144]{0:T(1024)S(1)}, u32[]{:S(2)}, u32[]{:S(2)}) collective-permute-start(f32[262144]{0:T(1024)S(1)} %add.57), channel_id=1, source_target_pairs={{0,8},{4,12},{8,0},{12,4},{16,24},{20,28},{24,16},{28,20},{1,9},{5... | collective-permute-start | bytes 3145736 | tf_op jit(solution)/shard_map/ppermute | solution.py:27
  194.0 45.8 %collective-permute-start.5 = (f32[262144]{0:T(1024)S(1)}, f32[262144]{0:T(1024)S(1)}, u32[]{:S(2)}, u32[]{:S(2)}) collective-permute-start(f32[262144]{0:T(1024)S(1)} %add.58), channel_id=1, source_target_pairs={{0,16},{4,20},{8,24},{12,28},{16,0},{20,4},{24,8},{28,12},{1,17},{... | collective-permute-start | bytes 3145736 | tf_op jit(solution)/shard_map/ppermute | solution.py:27
  263.6 24.3 %collective-permute-start.6 = (f32[262144]{0:T(1024)S(1)}, f32[262144]{0:T(1024)S(1)}, u32[]{:S(2)}, u32[]{:S(2)}) collective-permute-start(f32[262144]{0:T(1024)S(1)} %fusion.7), channel_id=1, source_target_pairs={{0,4},{4,0},{8,12},{12,8},{16,20},{20,16},{24,28},{28,24},{1,5},{5... | collective-permute-start | bytes 3145736 | tf_op jit(solution)/shard_map/ppermute | solution.py:27
  288.0 23.5 %collective-permute-start.7 = (f32[262144]{0:T(1024)S(1)}, f32[262144]{0:T(1024)S(1)}, u32[]{:S(2)}, u32[]{:S(2)}) collective-permute-start(f32[262144]{0:T(1024)S(1)} %add.62), channel_id=1, source_target_pairs={{0,8},{4,12},{8,0},{12,4},{16,24},{20,28},{24,16},{28,20},{1,9},{5... | collective-permute-start | bytes 3145736 | tf_op jit(solution)/shard_map/ppermute | solution.py:27
  311.6 45.6 %collective-permute-start.8 = (f32[262144]{0:T(1024)S(1)}, f32[262144]{0:T(1024)S(1)}, u32[]{:S(2)}, u32[]{:S(2)}) collective-permute-start(f32[262144]{0:T(1024)S(1)} %add.63), channel_id=1, source_target_pairs={{0,16},{4,20},{8,24},{12,28},{16,0},{20,4},{24,8},{28,12},{1,17},{... | collective-permute-start | bytes 3145736 | tf_op jit(solution)/shard_map/ppermute | solution.py:27
